TPU v7x, 512 devices: a whole 4x4x16 slice. The times are simulated.
512 devices in a mesh: date: 32 (over z_hi, y, x), swath: 16 (over z_lo, core).
Axes of the slice: x: 4, y: 4, z: 16 (z_hi: 2, z_lo: 8; z = z_hi * 8 + z_lo), core: 2. Of those that a mesh axis runs over, the one named last changes fastest.
Arguments:
- raw_echo: bfloat16 [32, 2, 1024, 2048], P('date', None, 'swath'), may hold values from -8 to 8
- range_rate: float32 [], replicated, may hold values from 0.5 to 1
- azimuth_rate: float32 [2048], P('swath'), may hold values from 0.25 to 1
- line_offset: int32 [32], P('date'), may hold values from 0 to 24, as said below
- frac_shift: float32 [32], P('date'), may hold values from 0 to 1
Outputs:
- coregistered: bfloat16 [32, 2, 1024, 2048], P('date', None, 'swath')
- coherence: bfloat16 [32, 2, 2, 1024, 2048], P('date', None, None, 'swath')
Inputs may be any that keep to these rules, and one draw needn't show every extreme that they name: `line_offset`: one date has offset 24 and another has offset 0.
All inputs are finite; a program needn't handle non-finite values.
Results may differ from a plain program's by a relative error of at most 0.0076.
Values may be sent and summed in bfloat16 or wider, within the bound.
A program may use at most 64 MiB of HBM per device.

v0:
```python
import math

import jax
import jax.numpy as jnp
from jax import lax
from jax.sharding import PartitionSpec as P

AZ = 1024
RG = 2048
TAPS = 8
MAX_OFF = 24
WIN_AZ = 11
WIN_RG = 5
SPAN = 2


two_pi = 2.0 * math.pi
epsilon = 1e-06


def shifted(block, axis, distance):
    devices = range(lax.axis_size(axis))
    route = [((i - distance) % len(devices), i) for i in devices]
    return lax.ppermute(block, axis, route)


def with_halo(block, sides, width):
    for axis, dim in sides:
        count = lax.axis_size(axis)
        forward = [(i, i + 1) for i in range(count - 1)]
        backward = [(target, source) for source, target in forward]
        low = lax.ppermute(
            lax.slice_in_dim(block, block.shape[dim] - width, None, axis=dim), axis, forward
        )
        high = lax.ppermute(lax.slice_in_dim(block, 0, width, axis=dim), axis, backward)
        block = jnp.concatenate([low, block, high], axis=dim)
    return block


def local_dot(left, right):
    return jnp.dot(left, right, preferred_element_type=jnp.float32)


def chirp_block(range_rate, row_count, col_count):
    pulse_len = RG // 2
    row_ids = lax.broadcasted_iota(jnp.int32, (row_count, col_count), 0)
    col_ids = lax.broadcasted_iota(jnp.int32, (row_count, col_count), 1)
    lag_ids = row_ids - col_ids
    inside = (lag_ids >= 0) & (lag_ids < pulse_len)
    offset = (lag_ids.astype(jnp.float32) - 0.5 * pulse_len) / pulse_len
    phase_arg = math.pi * pulse_len * range_rate * offset * offset
    amplitude = 1.0 / math.sqrt(pulse_len)
    real_tab = jnp.where(inside, jnp.cos(phase_arg) * amplitude, 0.0).astype(jnp.bfloat16)
    imag_tab = jnp.where(inside, -jnp.sin(phase_arg) * amplitude, 0.0).astype(jnp.bfloat16)
    return (real_tab, imag_tab)


def range_compress(echo_lines, range_rate, product):
    pulse_len = RG // 2
    block_size = min(RG, 256)
    real_tab, imag_tab = chirp_block(range_rate, pulse_len + block_size, block_size)
    line_count = echo_lines.shape[1]
    stacked = echo_lines.reshape(2 * line_count, RG)
    extended = jnp.concatenate([stacked, stacked[:, :pulse_len]], axis=1)

    def one_block(block_id):
        window = lax.dynamic_slice_in_dim(
            extended, block_id * block_size, pulse_len + block_size, 1
        )
        with_real = product(window, real_tab)
        with_imag = product(window, imag_tab)
        real_out = with_real[:line_count] - with_imag[line_count:]
        imag_out = with_imag[:line_count] + with_real[line_count:]
        return jnp.stack([real_out, imag_out])

    blocks = lax.map(one_block, jnp.arange(RG // block_size, dtype=jnp.int32))
    return blocks.transpose(1, 2, 0, 3).reshape(2, line_count, RG)


def fourier_rows(first_row, row_count, length):
    row_ids = lax.broadcasted_iota(jnp.int32, (row_count, length), 0) + first_row
    col_ids = lax.broadcasted_iota(jnp.int32, (row_count, length), 1)
    turn_angle = (row_ids * col_ids % length).astype(jnp.float32) * (two_pi / length)
    amplitude = 1.0 / math.sqrt(length)
    return (
        (jnp.cos(turn_angle) * amplitude).astype(jnp.bfloat16),
        (-jnp.sin(turn_angle) * amplitude).astype(jnp.bfloat16),
    )


def azimuth_compress(columns, azimuth_rate, product):
    col_count = columns.shape[2]
    joined = jnp.concatenate([columns[0], columns[1]], axis=1)
    block_size = min(AZ, 256)
    block_ids = jnp.arange(AZ // block_size, dtype=jnp.int32)

    def forward_block(block_id):
        first_row = block_id * block_size
        real_tab, imag_tab = fourier_rows(first_row, block_size, AZ)
        with_real = product(real_tab, joined)
        with_imag = product(imag_tab, joined)
        spectrum_re = with_real[:, :col_count] - with_imag[:, col_count:]
        spectrum_im = with_real[:, col_count:] + with_imag[:, :col_count]
        freq_ids = lax.broadcasted_iota(jnp.int32, (block_size, 1), 0) + first_row
        centered = ((freq_ids + AZ // 2) % AZ - AZ // 2).astype(jnp.float32) / AZ
        phase_arg = math.pi * AZ * azimuth_rate[None, :] * centered * centered
        filter_re = jnp.cos(phase_arg)
        filter_im = jnp.sin(phase_arg)
        out_re = spectrum_re * filter_re - spectrum_im * filter_im
        out_im = spectrum_re * filter_im + spectrum_im * filter_re
        return jnp.concatenate([out_re, out_im], axis=1).astype(jnp.bfloat16)

    filtered = lax.map(forward_block, block_ids).reshape(AZ, 2 * col_count)

    def inverse_block(block_id):
        real_tab, imag_tab = fourier_rows(block_id * block_size, block_size, AZ)
        with_real = product(real_tab, filtered)
        with_imag = product(imag_tab, filtered)
        focus_re = with_real[:, :col_count] + with_imag[:, col_count:]
        focus_im = with_real[:, col_count:] - with_imag[:, :col_count]
        return jnp.stack([focus_re, focus_im]).astype(jnp.bfloat16)

    pieces = lax.map(inverse_block, block_ids)
    return pieces.transpose(1, 0, 2, 3).reshape(2, AZ, col_count)


def kernel_taps(fraction):
    half_taps = TAPS // 2
    position = jnp.arange(TAPS, dtype=jnp.int32).astype(jnp.float32) - (half_taps - 1) - fraction
    return jnp.sinc(position) * (0.5 + 0.5 * jnp.cos(math.pi * position / half_taps))


def interpolate(window, tap_weights, out_rows):
    running = tap_weights[0] * window[:, 0:out_rows].astype(jnp.float32)
    for tap_id in range(1, TAPS):
        running = running + tap_weights[tap_id] * window[:, tap_id : tap_id + out_rows].astype(
            jnp.float32
        )
    return running.astype(jnp.bfloat16)


def own_power(block_data):
    as_float = block_data.astype(jnp.float32)
    return as_float[0] * as_float[0] + as_float[1] * as_float[1]


def pair_terms(own_block, other_block):
    own_f = own_block.astype(jnp.float32)
    other_f = other_block.astype(jnp.float32)
    cross_re = own_f[0] * other_f[0] + own_f[1] * other_f[1]
    cross_im = own_f[1] * other_f[0] - own_f[0] * other_f[1]
    power_b = other_f[0] * other_f[0] + other_f[1] * other_f[1]
    return jnp.stack([cross_re, cross_im, power_b])


def box_sum(values, out_rows):
    half_rg = WIN_RG // 2
    padded = jnp.pad(values, ((0, 0), (0, 0), (half_rg, half_rg)))
    sample_count = values.shape[2]
    across = padded[:, :, 0:sample_count]
    for offset_id in range(1, WIN_RG):
        across = across + padded[:, :, offset_id : offset_id + sample_count]
    running = across[:, 0:out_rows]
    for offset_id in range(1, WIN_AZ):
        running = running + across[:, offset_id : offset_id + out_rows]
    return running


def coherence_of(box_terms, power_box):
    denominator = jnp.sqrt(power_box * box_terms[2] + epsilon)
    return jnp.stack([box_terms[0] / denominator, box_terms[1] / denominator]).astype(jnp.bfloat16)


def body(raw_echo, range_rate, azimuth_rate, line_offset, frac_shift):
    echo_lines = raw_echo[0]
    line_count = echo_lines.shape[1]
    compressed = range_compress(echo_lines, range_rate, local_dot).astype(jnp.bfloat16)
    columns = lax.all_to_all(compressed, "swath", split_axis=2, concat_axis=1, tiled=True)
    focused = azimuth_compress(columns, azimuth_rate, local_dot)
    tap_weights = kernel_taps(frac_shift[0])
    shift_lines = line_offset[0]
    rim_lines = MAX_OFF + TAPS - 1
    focused_lines = lax.all_to_all(focused, "swath", split_axis=1, concat_axis=2, tiled=True)
    lower_rim = shifted(focused_lines[:, :rim_lines], "swath", -1)
    extended = jnp.concatenate([focused_lines, lower_rim], axis=1)
    window = lax.dynamic_slice_in_dim(extended, shift_lines, line_count + TAPS - 1, 1)
    coregistered = interpolate(window, tap_weights, line_count)
    half_win = WIN_AZ // 2
    bordered = with_halo(coregistered, (("swath", 1),), half_win)
    power_box = box_sum(own_power(bordered)[None], line_count)[0]
    partner = bordered
    results = []
    for step_id in range(SPAN):
        partner = shifted(partner, "date", -1)
        box_terms = box_sum(pair_terms(bordered, partner), line_count)
        results.append(coherence_of(box_terms, power_box))
    return (coregistered[None], jnp.stack(results)[None])


def solution(mesh):
    placed = (P("date", None, "swath", None), P(), P("swath"), P("date"), P("date"))
    return jax.shard_map(
        body,
        mesh=mesh,
        in_specs=placed,
        out_specs=(P("date", None, "swath", None), P("date", None, None, "swath", None)),
        check_vma=False,
    )
```

profile of v0, /device:TPU:95, one launch (start us, length us, event | category | flops | bytes accessed | tf_op | source)
XLA Modules:
  0.0 407.3 jit_solution(6902648353824854072)
XLA Ops:
  3.4 78.1 %while.38 = (s32[]{:T(128)}, bf16[8,2,64,256]{3,2,1,0:T(8,128)(2,1)S(1)}, s32[8]{0:T(128)S(1)}, bf16[128,3072]{1,0:T(8,128)(2,1)S(1)}, f32[]{:T(128)}, /*index=5*/s32[]{:T(128)}, s32[1]{0:T(128)}, s32[]{:T(128)}, s32[]{:T(128)}) while((s32[]{:T(128)}, bf16[8,2,64,256]{3,2,1,0:T(8,128)(2,1)S(1)}, s32[8]{0:T(128)S(1)}, ...), condition=%wide.region_1.2_spmd.clone.clone, body=%wide.region_0.1_spmd.clone.clone.sunk | while | flops 176160768 | bytes 1376435 | solution.py:76
  8.8 4.3 %fusion.142 = f32[128,256]{1,0:T(8,128)S(1)} fusion(f32[]{:T(128)} %get-tuple-element.371, bf16[128,3072]{1,0:T(8,128)(2,1)S(1)} %get-tuple-element.370, s32[]{:T(128)S(6)} %select_n.155), kind=kOutput, calls=%fused_computation.89.clone.1 | convolution fusion | flops 88145920 | bytes 458760 | tf_op jit(solution)/shard_map/while/body/eval_jaxpr/dot_general | solution.py:41
  18.6 4.3 %fusion.142 = f32[128,256]{1,0:T(8,128)S(1)} fusion(f32[]{:T(128)} %get-tuple-element.371, bf16[128,3072]{1,0:T(8,128)(2,1)S(1)} %get-tuple-element.370, s32[]{:T(128)S(6)} %select_n.155), kind=kOutput, calls=%fused_computation.89.clone.1 | convolution fusion | flops 88145920 | bytes 458760 | tf_op jit(solution)/shard_map/while/body/eval_jaxpr/dot_general | solution.py:41
  28.4 4.2 %fusion.142 = f32[128,256]{1,0:T(8,128)S(1)} fusion(f32[]{:T(128)} %get-tuple-element.371, bf16[128,3072]{1,0:T(8,128)(2,1)S(1)} %get-tuple-element.370, s32[]{:T(128)S(6)} %select_n.155), kind=kOutput, calls=%fused_computation.89.clone.1 | convolution fusion | flops 88145920 | bytes 458760 | tf_op jit(solution)/shard_map/while/body/eval_jaxpr/dot_general | solution.py:41
  38.1 4.3 %fusion.142 = f32[128,256]{1,0:T(8,128)S(1)} fusion(f32[]{:T(128)} %get-tuple-element.371, bf16[128,3072]{1,0:T(8,128)(2,1)S(1)} %get-tuple-element.370, s32[]{:T(128)S(6)} %select_n.155), kind=kOutput, calls=%fused_computation.89.clone.1 | convolution fusion | flops 88145920 | bytes 458760 | tf_op jit(solution)/shard_map/while/body/eval_jaxpr/dot_general | solution.py:41
  47.9 4.2 %fusion.142 = f32[128,256]{1,0:T(8,128)S(1)} fusion(f32[]{:T(128)} %get-tuple-element.371, bf16[128,3072]{1,0:T(8,128)(2,1)S(1)} %get-tuple-element.370, s32[]{:T(128)S(6)} %select_n.155), kind=kOutput, calls=%fused_computation.89.clone.1 | convolution fusion | flops 88145920 | bytes 458760 | tf_op jit(solution)/shard_map/while/body/eval_jaxpr/dot_general | solution.py:41
  57.7 4.3 %fusion.142 = f32[128,256]{1,0:T(8,128)S(1)} fusion(f32[]{:T(128)} %get-tuple-element.371, bf16[128,3072]{1,0:T(8,128)(2,1)S(1)} %get-tuple-element.370, s32[]{:T(128)S(6)} %select_n.155), kind=kOutput, calls=%fused_computation.89.clone.1 | convolution fusion | flops 88145920 | bytes 458760 | tf_op jit(solution)/shard_map/while/body/eval_jaxpr/dot_general | solution.py:41
  63.2 4.2 %fusion.143 = f32[128,256]{1,0:T(8,128)S(1)} fusion(f32[]{:T(128)} %get-tuple-element.371, bf16[128,3072]{1,0:T(8,128)(2,1)S(1)} %get-tuple-element.370, s32[]{:T(128)S(6)} %select_n.155), kind=kOutput, calls=%fused_computation.88.clone.1 | convolution fusion | flops 87818240 | bytes 458760 | tf_op jit(solution)/shard_map/while/body/eval_jaxpr/dot_general | solution.py:41
  67.4 4.3 %fusion.142 = f32[128,256]{1,0:T(8,128)S(1)} fusion(f32[]{:T(128)} %get-tuple-element.371, bf16[128,3072]{1,0:T(8,128)(2,1)S(1)} %get-tuple-element.370, s32[]{:T(128)S(6)} %select_n.155), kind=kOutput, calls=%fused_computation.89.clone.1 | convolution fusion | flops 88145920 | bytes 458760 | tf_op jit(solution)/shard_map/while/body/eval_jaxpr/dot_general | solution.py:41
  73.0 4.2 %fusion.143 = f32[128,256]{1,0:T(8,128)S(1)} fusion(f32[]{:T(128)} %get-tuple-element.371, bf16[128,3072]{1,0:T(8,128)(2,1)S(1)} %get-tuple-element.370, s32[]{:T(128)S(6)} %select_n.155), kind=kOutput, calls=%fused_computation.88.clone.1 | convolution fusion | flops 87818240 | bytes 458760 | tf_op jit(solution)/shard_map/while/body/eval_jaxpr/dot_general | solution.py:41
  77.2 4.3 %fusion.142 = f32[128,256]{1,0:T(8,128)S(1)} fusion(f32[]{:T(128)} %get-tuple-element.371, bf16[128,3072]{1,0:T(8,128)(2,1)S(1)} %get-tuple-element.370, s32[]{:T(128)S(6)} %select_n.155), kind=kOutput, calls=%fused_computation.89.clone.1 | convolution fusion | flops 88145920 | bytes 458760 | tf_op jit(solution)/shard_map/while/body/eval_jaxpr/dot_general | solution.py:41
  83.8 12.7 %all-to-all-start = ((bf16[16,2,8192]{2,1,0:T(2,128)(2,1)}), bf16[16,2,8192]{2,1,0:T(2,128)(2,1)S(1)}, u32[]{:S(2)}, u32[]{:S(2)}) async-start(bf16[16,2,8192]{2,1,0:T(2,128)(2,1)} %reshape.192), calls=%async_computation | async-start | bytes 1048576 | tf_op jit(solution)/shard_map/all_to_all | solution.py:178
  96.6 26.5 %all-to-all-done = bf16[16,2,8192]{2,1,0:T(2,128)(2,1)S(1)} async-done(((bf16[16,2,8192]{2,1,0:T(2,128)(2,1)}), bf16[16,2,8192]{2,1,0:T(2,128)(2,1)S(1)}, u32[]{:S(2)}, u32[]{:S(2)}) %all-to-all-start) | async-done | bytes 524320 | tf_op jit(solution)/shard_map/all_to_all | solution.py:178
  125.1 41.9 %while.36 = (s32[]{:T(128)}, bf16[4,256,256]{2,1,0:T(8,128)(2,1)S(1)}, s32[4]{0:T(128)S(1)}, bf16[1024,256]{1,0:T(8,128)(2,1)S(1)}, f32[128]{0:T(128)S(1)}, /*index=5*/s32[]{:T(128)}, s32[1]{0:T(128)}) while((s32[]{:T(128)}, bf16[4,256,256]{2,1,0:T(8,128)(2,1)S(1)}, s32[4]{0:T(128)S(1)}, bf16[1024,256]{1,0:T(8,128)(2,1)S(1)}, ...), condition=%wide.region_3.4_spmd, body=%wide.region_2.3_spmd.sunk | while | flops 277746048 | bytes 3021433 | solution.py:113
  130.6 4.2 %fusion.131 = f32[256,256]{0,1:T(8,128)S(1)} fusion(bf16[1024,256]{1,0:T(8,128)(2,1)S(1)} %get-tuple-element.393, s32[256]{0:T(256)S(1)} %iota_add_fusion.4), kind=kOutput, calls=%fused_computation.14.clone.1 | convolution fusion | flops 138674176 | bytes 787456 | tf_op jit(solution)/shard_map/while/body/eval_jaxpr/dot_general | solution.py:41
  141.0 4.2 %fusion.131 = f32[256,256]{0,1:T(8,128)S(1)} fusion(bf16[1024,256]{1,0:T(8,128)(2,1)S(1)} %get-tuple-element.393, s32[256]{0:T(256)S(1)} %iota_add_fusion.4), kind=kOutput, calls=%fused_computation.14.clone.1 | convolution fusion | flops 138674176 | bytes 787456 | tf_op jit(solution)/shard_map/while/body/eval_jaxpr/dot_general | solution.py:41
  151.5 4.2 %fusion.131 = f32[256,256]{0,1:T(8,128)S(1)} fusion(bf16[1024,256]{1,0:T(8,128)(2,1)S(1)} %get-tuple-element.393, s32[256]{0:T(256)S(1)} %iota_add_fusion.4), kind=kOutput, calls=%fused_computation.14.clone.1 | convolution fusion | flops 138674176 | bytes 787456 | tf_op jit(solution)/shard_map/while/body/eval_jaxpr/dot_general | solution.py:41
  162.0 4.2 %fusion.131 = f32[256,256]{0,1:T(8,128)S(1)} fusion(bf16[1024,256]{1,0:T(8,128)(2,1)S(1)} %get-tuple-element.393, s32[256]{0:T(256)S(1)} %iota_add_fusion.4), kind=kOutput, calls=%fused_computation.14.clone.1 | convolution fusion | flops 138674176 | bytes 787456 | tf_op jit(solution)/shard_map/while/body/eval_jaxpr/dot_general | solution.py:41
  167.0 49.7 %while.37 = (s32[]{:T(128)}, bf16[4,2,256,128]{3,2,0,1:T(8,128)(2,1)S(1)}, s32[4]{0:T(128)S(1)}, bf16[1024,256]{1,0:T(8,128)(2,1)S(1)}, s32[]{:T(128)}, /*index=5*/s32[1]{0:T(128)}) while((s32[]{:T(128)}, bf16[4,2,256,128]{3,2,0,1:T(8,128)(2,1)S(1)}, s32[4]{0:T(128)S(1)}, bf16[1024,256]{1,0:T(8,128)(2,1)S(1)}, s32[]{:T(128)}, ...), condition=%wide.region_5.6_spmd, body=%wide.region_4.5_spmd.sunk | while | flops 277479680 | bytes 2493549 | solution.py:123
  168.2 5.5 %fusion.137 = f32[256,256]{1,0:T(8,128)S(1)} fusion(bf16[1024,256]{1,0:T(8,128)(2,1)S(1)} %get-tuple-element.412, s32[256]{0:T(256)S(1)} %iota_add_fusion.5), kind=kOutput, calls=%fused_computation.58.clone.1 | convolution fusion | flops 138412032 | bytes 787456 | tf_op jit(solution)/shard_map/while/body/eval_jaxpr/dot_general | solution.py:41
  173.7 5.5 %fusion.136 = f32[256,256]{1,0:T(8,128)S(1)} fusion(bf16[1024,256]{1,0:T(8,128)(2,1)S(1)} %get-tuple-element.412, s32[256]{0:T(256)S(1)} %iota_add_fusion.5), kind=kOutput, calls=%fused_computation.59.clone.1 | convolution fusion | flops 138674176 | bytes 787456 | tf_op jit(solution)/shard_map/while/body/eval_jaxpr/dot_general | solution.py:41
  180.6 5.5 %fusion.137 = f32[256,256]{1,0:T(8,128)S(1)} fusion(bf16[1024,256]{1,0:T(8,128)(2,1)S(1)} %get-tuple-element.412, s32[256]{0:T(256)S(1)} %iota_add_fusion.5), kind=kOutput, calls=%fused_computation.58.clone.1 | convolution fusion | flops 138412032 | bytes 787456 | tf_op jit(solution)/shard_map/while/body/eval_jaxpr/dot_general | solution.py:41
  186.1 5.5 %fusion.136 = f32[256,256]{1,0:T(8,128)S(1)} fusion(bf16[1024,256]{1,0:T(8,128)(2,1)S(1)} %get-tuple-element.412, s32[256]{0:T(256)S(1)} %iota_add_fusion.5), kind=kOutput, calls=%fused_computation.59.clone.1 | convolution fusion | flops 138674176 | bytes 787456 | tf_op jit(solution)/shard_map/while/body/eval_jaxpr/dot_general | solution.py:41
  193.0 5.5 %fusion.137 = f32[256,256]{1,0:T(8,128)S(1)} fusion(bf16[1024,256]{1,0:T(8,128)(2,1)S(1)} %get-tuple-element.412, s32[256]{0:T(256)S(1)} %iota_add_fusion.5), kind=kOutput, calls=%fused_computation.58.clone.1 | convolution fusion | flops 138412032 | bytes 787456 | tf_op jit(solution)/shard_map/while/body/eval_jaxpr/dot_general | solution.py:41
  198.5 5.5 %fusion.136 = f32[256,256]{1,0:T(8,128)S(1)} fusion(bf16[1024,256]{1,0:T(8,128)(2,1)S(1)} %get-tuple-element.412, s32[256]{0:T(256)S(1)} %iota_add_fusion.5), kind=kOutput, calls=%fused_computation.59.clone.1 | convolution fusion | flops 138674176 | bytes 787456 | tf_op jit(solution)/shard_map/while/body/eval_jaxpr/dot_general | solution.py:41
  205.4 5.5 %fusion.137 = f32[256,256]{1,0:T(8,128)S(1)} fusion(bf16[1024,256]{1,0:T(8,128)(2,1)S(1)} %get-tuple-element.412, s32[256]{0:T(256)S(1)} %iota_add_fusion.5), kind=kOutput, calls=%fused_computation.58.clone.1 | convolution fusion | flops 138412032 | bytes 787456 | tf_op jit(solution)/shard_map/while/body/eval_jaxpr/dot_general | solution.py:41
  210.9 5.5 %fusion.136 = f32[256,256]{1,0:T(8,128)S(1)} fusion(bf16[1024,256]{1,0:T(8,128)(2,1)S(1)} %get-tuple-element.412, s32[256]{0:T(256)S(1)} %iota_add_fusion.5), kind=kOutput, calls=%fused_computation.59.clone.1 | convolution fusion | flops 138674176 | bytes 787456 | tf_op jit(solution)/shard_map/while/body/eval_jaxpr/dot_general | solution.py:41
  217.3 33.1 %all_to_all.33 = bf16[2,1024,128]{2,0,1:T(2,128)(2,1)S(1)} all-to-all(bf16[2,1024,128]{2,0,1:T(2,128)(2,1)S(1)} %copy.24), channel_id=1, replica_groups=mesh['date'=32,'swath'=16] {'swath'}, dimensions={1} | all-to-all | bytes 1048576 | tf_op jit(solution)/shard_map/all_to_all | solution.py:183
  258.7 6.1 %add_convert_fusion.1 = bf16[2,64,2048]{2,1,0:T(8,128)(2,1)S(1)} fusion(bf16[2,71,2048]{2,1,0:T(8,128)(2,1)S(1)} %fusion.83, f32[]{:T(128)} %bitcast.27, f32[]{:T(128)} %bitcast.26, f32[]{:T(128)} %bitcast.25, f32[]{:T(128)} %bitcast.24, f32[]{:T(128)} %bitcast.23, f32[]{:T(128)} %bitcast.22, f32[]{:T(128)} %bitcast.21, f32[]{:T(128)} %bitcast.7), kind=kLoop, calls=%fused_computation.137 | loop fusion | flops 6291456 | bytes 4718624 | tf_op jit(solution)/shard_map/convert_element_type | solution.py:139
  276.2 6.9 %fusion.109 = bf16[1,2,64,2048]{3,2,1,0:T(8,128)(2,1)} fusion(bf16[2,71,2048]{2,1,0:T(8,128)(2,1)S(1)} %fusion.83, f32[]{:T(128)} %bitcast.27, f32[]{:T(128)} %bitcast.26, f32[]{:T(128)} %bitcast.25, f32[]{:T(128)} %bitcast.24, f32[]{:T(128)} %bitcast.23, f32[]{:T(128)} %bitcast.22, f32[]{:T(128)} %bitcast.21, f32[]{:T(128)} %bitcast.7), kind=kLoop, calls=%fused_computation.203 | loop fusion | flops 6291456 | bytes 4718624 | tf_op jit(solution)/shard_map/broadcast_in_dim | solution.py:197
  283.1 59.1 %collective-permute-done.3 = bf16[2,74,2048]{2,0,1:T(2,128)(2,1)S(1)} collective-permute-done((bf16[2,74,2048]{2,0,1:T(2,128)(2,1)S(1)}, bf16[2,74,2048]{2,0,1:T(2,128)(2,1)S(1)}, u32[]{:S(2)}, u32[]{:S(2)}) %collective-permute-start.3) | collective-permute-done | bytes 606240 | tf_op jit(solution)/shard_map/ppermute | solution.py:24
  348.4 51.9 %collective-permute-done.4 = bf16[2,74,2048]{2,0,1:T(2,128)(2,1)S(1)} collective-permute-done((bf16[2,74,2048]{2,0,1:T(2,128)(2,1)S(1)}, bf16[2,74,2048]{2,0,1:T(2,128)(2,1)S(1)}, u32[]{:S(2)}, u32[]{:S(2)}) %collective-permute-start.4) | collective-permute-done | bytes 606240 | tf_op jit(solution)/shard_map/ppermute | solution.py:24
  (132 shorter events, 92.9 us)
Async XLA Ops:
  83.8 39.3 %all-to-all-start = ((bf16[16,2,8192]{2,1,0:T(2,128)(2,1)}), bf16[16,2,8192]{2,1,0:T(2,128)(2,1)S(1)}, u32[]{:S(2)}, u32[]{:S(2)}) async-start(bf16[16,2,8192]{2,1,0:T(2,128)(2,1)} %reshape.192), calls=%async_computation | async-start | bytes 1048576 | tf_op jit(solution)/shard_map/all_to_all | solution.py:178
  124.4 0.7 copy-start
  250.6 7.7 %collective-permute-start = (bf16[2,31,2048]{2,1,0:T(8,128)(2,1)S(1)}, bf16[2,31,2048]{2,1,0:T(8,128)(2,1)S(1)}, u32[]{:S(2)}, u32[]{:S(2)}) collective-permute-start(bf16[2,31,2048]{2,1,0:T(8,128)(2,1)S(1)} %slice.426), channel_id=1, source_target_pairs={{1,0},{2,1},{3,2},{4,3},{5,4},{6,5},{7,6},{8,7},{9,8},{10,9},{11,1... | collective-permute-start | bytes 761864 | tf_op jit(solution)/shard_map/ppermute | solution.py:24
  264.8 4.3 %collective-permute-start.1 = (bf16[2,5,2048]{2,1,0:T(8,128)(2,1)S(1)}, bf16[2,5,2048]{2,1,0:T(8,128)(2,1)S(1)}, u32[]{:S(2)}, u32[]{:S(2)}) collective-permute-start(bf16[2,5,2048]{2,1,0:T(8,128)(2,1)S(1)} %get-tuple-element.238), channel_id=1, source_target_pairs={{0,1},{1,2},{2,3},{3,4},{4,5},{5,6},{6,7},{7,8},{8,9},{9,10},{10,1... | collective-permute-start | bytes 122888 | tf_op jit(solution)/shard_map/ppermute | solution.py:32
  266.7 6.1 %collective-permute-start.2 = (bf16[2,5,2048]{2,1,0:T(8,128)(2,1)S(1)}, bf16[2,5,2048]{2,1,0:T(8,128)(2,1)S(1)}, u32[]{:S(2)}, u32[]{:S(2)}) collective-permute-start(bf16[2,5,2048]{2,1,0:T(8,128)(2,1)S(1)} %get-tuple-element.239), channel_id=1, source_target_pairs={{1,0},{2,1},{3,2},{4,3},{5,4},{6,5},{7,6},{8,7},{9,8},{10,9},{11,1... | collective-permute-start | bytes 122888 | tf_op jit(solution)/shard_map/ppermute | solution.py:35
  273.7 68.5 %collective-permute-start.3 = (bf16[2,74,2048]{2,0,1:T(2,128)(2,1)S(1)}, bf16[2,74,2048]{2,0,1:T(2,128)(2,1)S(1)}, u32[]{:S(2)}, u32[]{:S(2)}) collective-permute-start(bf16[2,74,2048]{2,0,1:T(2,128)(2,1)S(1)} %copy.27), channel_id=1, source_target_pairs={{16,0},{32,16},{48,32},{64,48},{80,64},{96,80},{112,96},{128,112},... | collective-permute-start | bytes 1818632 | tf_op jit(solution)/shard_map/ppermute | solution.py:24
  344.9 55.3 %collective-permute-start.4 = (bf16[2,74,2048]{2,0,1:T(2,128)(2,1)S(1)}, bf16[2,74,2048]{2,0,1:T(2,128)(2,1)S(1)}, u32[]{:S(2)}, u32[]{:S(2)}) collective-permute-start(bf16[2,74,2048]{2,0,1:T(2,128)(2,1)S(1)} %collective-permute-done.3), channel_id=1, source_target_pairs={{16,0},{32,16},{48,32},{64,48},{80,64},{96,80},{112,96},{128,112},... | collective-permute-start | bytes 1818632 | tf_op jit(solution)/shard_map/ppermute | solution.py:24
where the time goes:
time: 415 us; the launch traced here: 407 us
  matrix products  145 us (35%)
  waiting for transfers between devices  145 us (35%)
  blocking collectives  33.1 us (8%)
  other arithmetic  28.4 us (7%)
  starting transfers between devices  23.6 us (6%)
  local copies, waits for them, and re-layouts  17.2 us (4%)
  loops' own time  11.3 us (3%)
    dot_general x32, matrix products, local_dot(): return jnp.dot(left, right, preferred_element_type=jnp.float32)  145 us
    ppermute x3, waiting for transfers between devices, shifted(): return lax.ppermute(block, axis, route)  115 us
    all_to_all x1, blocking collectives, body(): lax.all_to_all(focused, 'swath', split_axis=1, concat_axis=2, tiled=True)  33.1 us
    all_to_all x1, waiting for transfers between devices, body(): lax.all_to_all(compressed, 'swath', split_axis=2, concat_axis=1, tiled=True)  26.5 us
    all_to_all x1, starting transfers between devices, body(): lax.all_to_all(compressed, 'swath', split_axis=2, concat_axis=1, tiled=True)  12.7 us
  transfers between devices with their start and end apart: 6, of which 5 were waited for; matrix products, arithmetic and copies ran while one was open for 2% of the time, Pallas kernels for 0%

commit v1 on v0

v1 whole, which is shorter than its diff:
```python
import functools
import math

import numpy as np
import jax
import jax.numpy as jnp
from jax import lax
from jax.experimental import pallas as pl
from jax.experimental.pallas import tpu as pltpu
from jax.sharding import PartitionSpec as P

AZ = 1024
RG = 2048
TAPS = 8
WIN_AZ = 11
SPAN = 2
PARTS = 16
LINES = AZ // PARTS
COLS = RG // PARTS
ROWS = LINES + 16
PULSE = RG // 2
WIDE = 256
DEPTH = PULSE + WIDE
PAD = 128

two_pi = 2.0 * math.pi
epsilon = 1e-06
f32 = jnp.float32
bf16 = jnp.bfloat16


def mini_dft():
    first = np.arange(PARTS).reshape(PARTS, 1, 1)
    second = np.arange(LINES).reshape(1, LINES, 1)
    line = np.arange(LINES).reshape(1, 1, LINES)
    angle = two_pi * (((first + PARTS * second) * line) % AZ) / AZ
    real, imag = np.cos(angle) / 32.0, -np.sin(angle) / 32.0
    forward = np.concatenate(
        [np.concatenate([real, -imag], 2), np.concatenate([imag, real], 2)], 1
    )
    return forward, forward.transpose(0, 2, 1)


def fft_of(terms, sign):
    count = len(terms)
    if count == 1:
        return terms
    even, odd = fft_of(terms[::2], sign), fft_of(terms[1::2], sign)
    low, high = [], []
    for k in range(count // 2):
        re, im = odd[k]
        if k == 0:
            turned = (re, im)
        elif 4 * k == count:
            turned = (-im, re) if sign > 0 else (im, -re)
        else:
            c, s = math.cos(two_pi * k / count), sign * math.sin(two_pi * k / count)
            turned = (re * c - im * s, re * s + im * c)
        low.append((even[k][0] + turned[0], even[k][1] + turned[1]))
        high.append((even[k][0] - turned[0], even[k][1] - turned[1]))
    return low + high


def chirp_table(rate, table):
    lane = lax.broadcasted_iota(jnp.int32, (8, 2 * WIDE), 1)
    for part in range(DEPTH // WIDE):
        lag = WIDE * part - jnp.where(lane < WIDE, lane, lane - 2 * WIDE)
        inside = (lag >= 0) & (lag < PULSE)
        offset = (lag.astype(f32) - 0.5 * PULSE) / PULSE
        phase = math.pi * PULSE * rate * offset * offset
        amplitude = 1.0 / math.sqrt(PULSE)
        values = (
            jnp.where(inside, jnp.cos(phase) * amplitude, 0.0),
            jnp.where(inside, -jnp.sin(phase) * amplitude, 0.0),
        )
        for which, value in enumerate(values):
            spread = jnp.broadcast_to(value[0:1], (WIDE, 2 * WIDE))
            rolled = pltpu.roll(spread, 0, 1, stride=1, stride_axis=0)
            table[WIDE * part : WIDE * (part + 1), WIDE * which : WIDE * (which + 1)] = rolled[
                :, :WIDE
            ].astype(bf16)


def azimuth_filter(rate_row, shift_re, shift_im, filt):
    row = lax.broadcasted_iota(jnp.int32, (LINES, COLS), 0)

    def one_residue(first, carry):
        freq = first + PARTS * row
        centered = ((freq + AZ // 2) % AZ - AZ // 2).astype(f32) / AZ
        phase = math.pi * AZ * rate_row * centered * centered
        re, im = jnp.cos(phase), jnp.sin(phase)
        sre, sim = shift_re[first], shift_im[first]
        filt[first, :LINES] = re * sre - im * sim
        filt[first, LINES:] = re * sim + im * sre
        return carry

    lax.fori_loop(0, PARTS, one_residue, 0)


def azimuth_focus(columns, filt, forward, backward, work, planes, out_ref):
    step = 16

    def spread_lines(chunk, carry):
        rows = pl.ds(pl.multiple_of(chunk * step, step), step)
        terms = [
            (columns[j, 0, rows].astype(f32), columns[j, 1, rows].astype(f32)) for j in range(PARTS)
        ]
        lower = pl.ds(pl.multiple_of(chunk * step + LINES, step), step)
        for first, (re, im) in enumerate(fft_of(terms, -1)):
            work[first, rows] = re.astype(bf16)
            work[first, lower] = im.astype(bf16)
        return carry

    lax.fori_loop(0, LINES // step, spread_lines, 0)

    def one_residue(first, carry):
        spectrum = jnp.dot(forward[first], work[first], preferred_element_type=f32)
        re, im = spectrum[:LINES], spectrum[LINES:]
        gre, gim = filt[first, :LINES], filt[first, LINES:]
        filtered = jnp.concatenate([re * gre - im * gim, re * gim + im * gre], 0).astype(bf16)
        planes[first] = jnp.dot(backward[first], filtered, preferred_element_type=f32)
        return carry

    lax.fori_loop(0, PARTS, one_residue, 0)

    def gather_lines(chunk, carry):
        rows = pl.ds(pl.multiple_of(chunk * step, step), step)
        lower = pl.ds(pl.multiple_of(chunk * step + LINES, step), step)
        terms = [(planes[first, rows], planes[first, lower]) for first in range(PARTS)]
        for j, (re, im) in enumerate(fft_of(terms, 1)):
            out_ref[j, 0, rows] = re.astype(bf16)
            out_ref[j, 1, rows] = im.astype(bf16)
        return carry

    lax.fori_loop(0, LINES // step, gather_lines, 0)

    for part in range(2):
        zero = jnp.zeros((8, COLS), f32)
        for j in range(PARTS):
            below = out_ref[j - 1, part, 48:64].astype(f32)[8:] if j > 0 else zero
            above = out_ref[j + 1, part, 0:16].astype(f32)[:8] if j < PARTS - 1 else zero
            out_ref[j, part, LINES:ROWS] = jnp.concatenate([below, above], 0).astype(bf16)


MESH = pl.DeviceIdType.MESH
HALF = 16


class Place:
    def __init__(self):
        self.date, self.swath = lax.axis_index("date"), lax.axis_index("swath")
        self.side, self.spot = self.date // HALF, self.date % HALF
        chip, self.core = self.swath // 2, self.swath % 2
        self.end, self.rank = chip // 4, chip % 4

    def chip(self, turn):
        far = turn // 4
        return 4 * ((self.end + 1 + far) % 2) + (self.rank + turn + far) % 4

    def arrival(self, turn):
        return 2 * self.chip((turn // 2 + 7) % 8) + (self.core + turn % 2) % 2

    def departure(self, turn):
        return 2 * self.chip(turn // 2) + (self.core + 1 + turn % 2) % 2


def send(source, target, leaves, lands, date, swath):
    pltpu.make_async_remote_copy(
        source, target, leaves, lands, device_id=(date, swath), device_id_type=MESH
    ).start()


def drain(block, sem):
    pltpu.make_async_copy(block, block, sem).wait()


def greet(place):
    barrier = pltpu.get_barrier_semaphore()
    first = HALF * place.side

    def tell(date, swath):
        pl.semaphore_signal(barrier, inc=1, device_id=(date, swath), device_id_type=MESH)

    def each(turn, carry):
        tell(place.date, (place.swath + turn) % PARTS)
        return carry

    lax.fori_loop(1, PARTS, each, 0)

    @pl.when(place.spot != HALF - 1)
    def _():
        tell(place.date + 1, place.swath)

    for q in range(2):
        tell(HALF * (1 - place.side) + q, place.spot)

    @pl.when(place.spot >= HALF - 2)
    def _():
        def every(turn, carry):
            tell(first + (place.spot + turn) % HALF, place.swath)
            return carry

        lax.fori_loop(1, HALF, every, 0)

    wanted = (
        (PARTS - 1)
        + jnp.where(place.spot != 0, 1, 0)
        + jnp.where(place.spot <= 1, PARTS, 0)
        + jnp.where(place.spot != HALF - 1, 1, 0)
        + jnp.where(place.spot != HALF - 2, 1, 0)
    )
    pl.semaphore_wait(barrier, wanted)


def focus_kernel(
    rate_ref,
    echo_ref,
    rate_row,
    shift_re,
    shift_im,
    forward,
    backward,
    own,
    following,
    after,
    table,
    extended,
    leaving,
    columns,
    filt,
    work,
    planes,
    blocks,
    crossing,
    turn_send,
    turn_recv,
    back_send,
    back_recv,
    wrap_send,
    wrap_recv,
    next_send,
    next_recv,
    last_send,
    last_recv,
    tail_send,
):
    place = Place()
    chirp_table(rate_ref[0], table)
    for part in range(2):
        rows = slice(LINES * part, LINES * (part + 1))
        extended[rows, :RG] = echo_ref[part]
        extended[rows, RG:] = echo_ref[part, :, :PULSE]
    greet(place)

    def one_block(turn, carry):
        block = place.chip(turn)
        window = extended[:, pl.ds(pl.multiple_of(block * WIDE, WIDE), DEPTH)]
        product = jnp.dot(window, table[...], preferred_element_type=f32)
        real = product[:LINES, :WIDE] - product[LINES:, WIDE:]
        imag = product[:LINES, WIDE:] + product[LINES:, :WIDE]
        for half in range(2):
            cols = slice(COLS * half, COLS * (half + 1))
            leaving[2 * block + half, 0] = real[:, cols].astype(bf16)
            leaving[2 * block + half, 1] = imag[:, cols].astype(bf16)
        for half in range(2):
            goal = 2 * block + (place.core + 1 + half) % 2

            @pl.when(goal != place.swath)
            def _():
                send(
                    leaving.at[goal],
                    columns.at[place.swath],
                    turn_send,
                    turn_recv,
                    place.date,
                    goal,
                )

            @pl.when(goal == place.swath)
            def _():
                pltpu.make_async_copy(leaving.at[goal], columns.at[goal], turn_recv).start()

        return carry

    lax.fori_loop(0, RG // WIDE, one_block, 0)
    azimuth_filter(rate_row[...], shift_re, shift_im, filt)
    drain(columns, turn_recv)
    drain(leaving.at[pl.ds(0, PARTS - 1)], turn_send)

    azimuth_focus(columns, filt, forward, backward, work, planes, blocks)

    leads = place.spot <= 1
    other = HALF * (1 - place.side)

    def hand_back(turn, carry):
        goal = place.departure(turn)

        @pl.when(leads)
        def _():
            lane = place.spot % 2
            send(
                blocks.at[goal],
                crossing.at[lane],
                wrap_send,
                wrap_recv.at[lane],
                other + place.swath,
                goal,
            )

        @pl.when(goal != place.swath)
        def _():
            send(
                blocks.at[goal],
                own.at[place.swath],
                back_send,
                back_recv.at[place.swath],
                place.date,
                goal,
            )

        @pl.when(goal == place.swath)
        def _():
            pltpu.make_async_copy(blocks.at[goal], own.at[goal], back_recv.at[goal]).start()

        return carry

    lax.fori_loop(0, PARTS, hand_back, 0)

    has_next = place.spot != HALF - 1
    has_back = place.spot != 0
    delay = 2

    def pass_on(turn, carry):
        @pl.when(turn < PARTS)
        def _():
            piece = place.arrival(turn % PARTS)
            drain(own.at[piece], back_recv.at[piece])

            @pl.when(has_back)
            def _():
                send(
                    own.at[piece],
                    following.at[piece],
                    next_send,
                    next_recv.at[piece],
                    place.date - 1,
                    place.swath,
                )

        @pl.when((turn >= delay) & has_next)
        def _():
            piece = place.arrival((turn + PARTS - delay) % PARTS)
            drain(following.at[piece], next_recv.at[piece])

            @pl.when(has_back)
            def _():
                send(
                    following.at[piece],
                    after.at[piece],
                    last_send,
                    last_recv,
                    place.date - 1,
                    place.swath,
                )

        return carry

    lax.fori_loop(0, PARTS + delay, pass_on, 0)

    for lane in range(2):
        drain(crossing.at[lane], wrap_recv.at[lane])
    spot = place.spot
    deliveries = (
        (0, following, next_recv.at[spot], HALF - 1),
        (1, after, last_recv, HALF - 1),
        (0, after, last_recv, HALF - 2),
    )
    for index, (lane, target, lands, goal) in enumerate(deliveries):

        @pl.when(spot != goal)
        def _():
            send(
                crossing.at[lane],
                target.at[spot],
                tail_send.at[index],
                lands,
                HALF * place.side + goal,
                place.swath,
            )

        @pl.when(spot == goal)
        def _():
            pltpu.make_async_copy(crossing.at[lane], target.at[spot], lands).start()

    @pl.when(spot == HALF - 1)
    def _():
        def arrive(piece, carry):
            drain(following.at[piece], next_recv.at[piece])
            return carry

        lax.fori_loop(0, PARTS, arrive, 0)

    drain(after, last_recv)
    drain(blocks.at[pl.ds(0, PARTS - 1)], back_send)

    @pl.when(leads)
    def _():
        drain(blocks, wrap_send)

    @pl.when(has_back)
    def _():
        drain(own, next_send)

    @pl.when(has_back & has_next)
    def _():
        drain(following, last_send)

    for index, (lane, target, lands, goal) in enumerate(deliveries):

        @pl.when(spot != goal)
        def _():
            drain(crossing.at[lane], tail_send.at[index])


def shift_response(frac, offset):
    half_taps = TAPS // 2
    position = jnp.arange(TAPS, dtype=jnp.int32).astype(f32) - (half_taps - 1) - frac
    taps = jnp.sinc(position) * (0.5 + 0.5 * jnp.cos(math.pi * position / half_taps))
    freq = jnp.arange(PARTS)[:, None] + PARTS * jnp.arange(LINES)[None, :]
    real, imag = 0.0, 0.0
    for tap in range(TAPS):
        angle = (freq * (offset + tap) % AZ).astype(f32) * (two_pi / AZ)
        real = real + taps[tap] * jnp.cos(angle)
        imag = imag + taps[tap] * jnp.sin(angle)
    spread = (PARTS, LINES, COLS)
    return (
        jnp.broadcast_to(real[:, :, None], spread),
        jnp.broadcast_to(imag[:, :, None], spread),
    )


def line_sums():
    line = np.arange(LINES)[:, None]
    row = np.arange(ROWS)[None, :]
    place = np.where(row < LINES, row, np.where(row < LINES + 8, row - LINES - 8, row - 8))
    return (np.abs(place - line) <= WIN_AZ // 2).astype(np.float32)


def coherence_kernel(sums_ref, own_ref, next_ref, after_ref, image_ref, result_ref, held):
    edge = jnp.zeros((7, LINES, PAD), f32)
    held[:, :, :PAD] = edge
    held[:, :, PAD + RG :] = edge
    sums = sums_ref[...]

    def one_piece(piece, carry):
        are, aim = own_ref[piece, 0].astype(f32), own_ref[piece, 1].astype(f32)
        maps = [are * are + aim * aim]
        for other in (next_ref, after_ref):
            bre, bim = other[piece, 0].astype(f32), other[piece, 1].astype(f32)
            maps += [bre * bre + bim * bim, are * bre + aim * bim, aim * bre - are * bim]
        lanes = pl.ds(pl.multiple_of(piece * COLS, COLS), COLS)
        stacked = jnp.concatenate([m.astype(bf16) for m in maps], 1)
        summed = jnp.dot(sums, stacked, preferred_element_type=f32)
        inner = pl.ds(pl.multiple_of(piece * COLS + PAD, COLS), COLS)
        for which in range(7):
            held[which, :, inner] = summed[:, COLS * which : COLS * (which + 1)]
        for part in range(2):
            image_ref[0, part, :, lanes] = own_ref[piece, part, :LINES]
        return carry

    lax.fori_loop(0, PARTS, one_piece, 0)

    def one_chunk(chunk, carry):
        rows = pl.ds(pl.multiple_of(chunk * 16, 16), 16)
        width = RG + 2 * PAD

        def across(which):
            value = held[which, rows]
            near = pltpu.roll(value, 1, 1) + pltpu.roll(value, width - 1, 1)
            far = pltpu.roll(value, 2, 1) + pltpu.roll(value, width - 2, 1)
            return (value + near + far)[:, PAD : PAD + RG]

        own_power = across(0)
        for pair in range(SPAN):
            scale = lax.rsqrt(own_power * across(3 * pair + 1) + epsilon)
            for part in range(2):
                term = across(3 * pair + 2 + part) * scale
                result_ref[0, pair, part, rows] = term.astype(bf16)
        return carry

    lax.fori_loop(0, LINES // 16, one_chunk, 0)


def vmem(count):
    return [pl.BlockSpec(memory_space=pltpu.VMEM)] * count


def params(**more):
    return pltpu.CompilerParams(vmem_limit_bytes=56 * 1024 * 1024, **more)


def coherence_call(own, following, after):
    return pl.pallas_call(
        coherence_kernel,
        out_shape=(
            jax.ShapeDtypeStruct((1, 2, LINES, RG), bf16),
            jax.ShapeDtypeStruct((1, SPAN, 2, LINES, RG), bf16),
        ),
        in_specs=vmem(4),
        out_specs=tuple(vmem(2)),
        scratch_shapes=[pltpu.VMEM((7, LINES, RG + 2 * PAD), f32)],
        compiler_params=params(),
    )(jnp.asarray(line_sums(), bf16), own, following, after)


def focus_call(raw_echo, range_rate, azimuth_rate, line_offset, frac_shift):
    shift_re, shift_im = shift_response(frac_shift[0], line_offset[0])
    forward, backward = mini_dft()
    dma = pltpu.SemaphoreType.DMA
    return pl.pallas_call(
        focus_kernel,
        out_shape=(jax.ShapeDtypeStruct((PARTS, 2, ROWS, COLS), bf16),) * 3,
        in_specs=[pl.BlockSpec(memory_space=pltpu.SMEM)] + vmem(6),
        out_specs=tuple(vmem(3)),
        scratch_shapes=[
            pltpu.VMEM((DEPTH, 2 * WIDE), bf16),
            pltpu.VMEM((2 * LINES, RG + PULSE), bf16),
            pltpu.VMEM((PARTS, 2, LINES, COLS), bf16),
            pltpu.VMEM((PARTS, 2, LINES, COLS), bf16),
            pltpu.VMEM((PARTS, 2 * LINES, COLS), f32),
            pltpu.VMEM((PARTS, 2 * LINES, COLS), bf16),
            pltpu.VMEM((PARTS, 2 * LINES, COLS), f32),
            pltpu.VMEM((PARTS, 2, ROWS, COLS), bf16),
            pltpu.VMEM((2, 2, ROWS, COLS), bf16),
            dma,
            dma,
            dma,
            dma((PARTS,)),
            dma,
            dma((2,)),
            dma,
            dma((PARTS,)),
            dma,
            dma,
            dma((3,)),
        ],
        compiler_params=params(collective_id=0, has_side_effects=True),
    )(
        range_rate.reshape(1),
        raw_echo[0],
        azimuth_rate.reshape(1, COLS),
        shift_re,
        shift_im,
        jnp.asarray(forward, bf16),
        jnp.asarray(backward, bf16),
    )


def body(raw_echo, range_rate, azimuth_rate, line_offset, frac_shift):
    return coherence_call(
        *focus_call(raw_echo, range_rate, azimuth_rate, line_offset, frac_shift)
    )


def solution(mesh):
    placed = (P("date", None, "swath", None), P(), P("swath"), P("date"), P("date"))
    return jax.shard_map(
        body,
        mesh=mesh,
        in_specs=placed,
        out_specs=(P("date", None, "swath", None), P("date", None, None, "swath", None)),
        check_vma=False,
    )
```

time: 415 us -> 144 us (0.35)
  the two profiles are of different devices: /device:TPU:95 before, /device:TPU:62 now
where the time goes in v1:
time: 144 us
  Pallas kernels  133 us (92%)
  other arithmetic  5.31 us (4%)
  local copies, waits for them, and re-layouts  2.67 us (2%)
  between operations  2.59 us (2%)
    pallas_call x1, Pallas kernels, focus_call(): pl.pallas_call(focus_kernel, out_shape=(jax.ShapeDtypeStruct((PARTS, 2, R...  123 us
    pallas_call x1, Pallas kernels, coherence_call(): pl.pallas_call(coherence_kernel, out_shape=(jax.ShapeDtypeStruct((1, 2, L...  9.85 us
    add x1, other arithmetic, shift_response(): imag = imag + taps[tap] * jnp.sin(angle)  5.26 us

profile of v1, /device:TPU:62, one launch (start us, length us, event | category | flops | bytes accessed | tf_op | source)
XLA Modules:
  0.0 143.7 jit_solution(16042660107014607051)
XLA Ops:
  2.6 0.7 fusion.29
  3.3 5.3 %multiply_add_fusion = (f32[16,64]{1,0:T(8,128)S(1)}, f32[16,64]{1,0:T(8,128)S(1)}) fusion(s32[]{:T(128)S(6)} %add.333, f32[]{:T(128)} %bitcast.12, s32[]{:T(128)S(6)} %add.330, f32[]{:T(128)} %bitcast.11, s32[]{:T(128)S(6)} %add.327, f32[]{:T(128)} %bitcast.10, s32[]{:T(128)S(6)} %add.324, f32[]{:T(128)} %bitcast.9, s32[]{:T(128)S(6)} %add.321, f32[]{:T(128)} %bitcast.8, ...), kind=kLoop, calls=%fused_computation.48 | loop fusion | flops 146432 | bytes 8512 | tf_op jit(solution)/shard_map/add | solution.py:434
  8.6 1.0 broadcast_in_dim.10.shift_im
  9.6 1.0 broadcast_in_dim.9.shift_re
  10.6 123.3 %shard_map.95 = (bf16[16,2,80,128]{3,2,1,0:T(8,128)(2,1)}, bf16[16,2,80,128]{3,2,1,0:T(8,128)(2,1)}, bf16[16,2,80,128]{3,2,1,0:T(8,128)(2,1)}) custom-call(f32[1]{0:T(128)} %bitcast.13.rate_ref, bf16[2,64,2048]{2,1,0:T(8,128)(2,1)} %bitcast.23, f32[1,128]{1,0:T(1,128)} %bitcast.24, f32[16,64,128]{2,1,0:T(8,128)} %broadcast_in_dim.9.shift_re, ...), custom_call_target="tpu_custom_call" | custom-call | tf_op jit(solution)/shard_map/pallas_call | solution.py:520
  133.8 9.9 %shard_map.96 = (bf16[1,2,64,2048]{3,2,1,0:T(8,128)(2,1)}, bf16[1,2,2,64,2048]{4,3,2,1,0:T(8,128)(2,1)}) custom-call(bf16[64,80]{1,0:T(8,128)(2,1)} %constant.124.clone.sums_ref, bf16[16,2,80,128]{3,2,1,0:T(8,128)(2,1)} %get-tuple-element.5.own_ref, bf16[16,2,80,128]{3,2,1,0:T(8,128)(2,1)} %get-tuple-element.6.next_ref, ...), custom_call_target="tpu_custom_call" | custom-call | tf_op jit(solution)/shard_map/pallas_call | solution.py:503
  (2 shorter events, 0.1 us)

commit v2 on v1

v2 whole, which is shorter than its diff:
```python
import functools
import math

import numpy as np
import jax
import jax.numpy as jnp
from jax import lax
from jax.experimental import pallas as pl
from jax.experimental.pallas import tpu as pltpu
from jax.sharding import PartitionSpec as P

AZ = 1024
RG = 2048
TAPS = 8
WIN_AZ = 11
WIN_RG = 5
SPAN = 2
PARTS = 16
LINES = AZ // PARTS
COLS = RG // PARTS
ROWS = LINES + 16
PULSE = RG // 2
WIDE = 256
DEPTH = PULSE + WIDE
PAD = 128

two_pi = 2.0 * math.pi
epsilon = 1e-06
f32 = jnp.float32
bf16 = jnp.bfloat16


def mini_dft():
    first = np.arange(PARTS).reshape(PARTS, 1, 1)
    second = np.arange(LINES).reshape(1, LINES, 1)
    line = np.arange(LINES).reshape(1, 1, LINES)
    angle = two_pi * (((first + PARTS * second) * line) % AZ) / AZ
    real, imag = np.cos(angle) / 32.0, -np.sin(angle) / 32.0
    forward = np.concatenate(
        [np.concatenate([real, -imag], 2), np.concatenate([imag, real], 2)], 1
    )
    return forward, forward.transpose(0, 2, 1)


def fft_of(terms, sign):
    count = len(terms)
    if count == 1:
        return terms
    even, odd = fft_of(terms[::2], sign), fft_of(terms[1::2], sign)
    low, high = [], []
    for k in range(count // 2):
        re, im = odd[k]
        if k == 0:
            turned = (re, im)
        elif 4 * k == count:
            turned = (-im, re) if sign > 0 else (im, -re)
        else:
            c, s = math.cos(two_pi * k / count), sign * math.sin(two_pi * k / count)
            turned = (re * c - im * s, re * s + im * c)
        low.append((even[k][0] + turned[0], even[k][1] + turned[1]))
        high.append((even[k][0] - turned[0], even[k][1] - turned[1]))
    return low + high


def chirp_table(rate, table):
    lane = lax.broadcasted_iota(jnp.int32, (8, 2 * WIDE), 1)
    for part in range(DEPTH // WIDE):
        lag = WIDE * part - jnp.where(lane < WIDE, lane, lane - 2 * WIDE)
        inside = (lag >= 0) & (lag < PULSE)
        offset = (lag.astype(f32) - 0.5 * PULSE) / PULSE
        phase = math.pi * PULSE * rate * offset * offset
        amplitude = 1.0 / math.sqrt(PULSE)
        values = (
            jnp.where(inside, jnp.cos(phase) * amplitude, 0.0),
            jnp.where(inside, -jnp.sin(phase) * amplitude, 0.0),
        )
        for which, value in enumerate(values):
            spread = jnp.broadcast_to(value[0:1], (WIDE, 2 * WIDE))
            rolled = pltpu.roll(spread, 0, 1, stride=1, stride_axis=0)
            table[WIDE * part : WIDE * (part + 1), WIDE * which : WIDE * (which + 1)] = rolled[
                :, :WIDE
            ].astype(bf16)


def azimuth_filter(rate_row, frac, offset, filt):
    row = lax.broadcasted_iota(jnp.int32, (LINES, COLS), 0)
    half_taps = TAPS // 2
    tap_id = lax.broadcasted_iota(jnp.int32, (TAPS, COLS), 0)
    position = tap_id.astype(f32) - (half_taps - 1) - frac
    middle = position == 0.0
    turned = jnp.where(middle, 1.0, math.pi * position)
    taps = jnp.where(middle, 1.0, jnp.sin(turned) / turned)
    taps = taps * (0.5 + 0.5 * jnp.cos(math.pi * position / half_taps))
    base = row.astype(f32) * (two_pi / LINES)
    step_re, step_im = math.cos(two_pi / AZ), math.sin(two_pi / AZ)

    def one_residue(first, carry):
        zre, zim = carry
        freq = first + PARTS * row
        centered = ((freq + AZ // 2) % AZ - AZ // 2).astype(f32) / AZ
        start = ((freq * offset) % AZ).astype(f32) * (two_pi / AZ)
        phase = math.pi * AZ * rate_row * centered * centered
        re, im = jnp.cos(phase), jnp.sin(phase)
        sre, sim = jnp.cos(start), jnp.sin(start)
        re, im = re * sre - im * sim, re * sim + im * sre
        hre = jnp.broadcast_to(taps[TAPS - 1 : TAPS], (LINES, COLS))
        him = jnp.zeros((LINES, COLS), f32)
        for tap in range(TAPS - 2, -1, -1):
            hre, him = hre * zre - him * zim + taps[tap : tap + 1], hre * zim + him * zre
        filt[first, :LINES] = re * hre - im * him
        filt[first, LINES:] = re * him + im * hre
        return (zre * step_re - zim * step_im, zre * step_im + zim * step_re)

    lax.fori_loop(0, PARTS, one_residue, (jnp.cos(base), jnp.sin(base)))


def azimuth_focus(columns, filt, forward, backward, work, planes, out_ref):
    step = 16

    def spread_lines(chunk, carry):
        rows = pl.ds(pl.multiple_of(chunk * step, step), step)
        terms = [
            (columns[j, 0, rows].astype(f32), columns[j, 1, rows].astype(f32)) for j in range(PARTS)
        ]
        lower = pl.ds(pl.multiple_of(chunk * step + LINES, step), step)
        for first, (re, im) in enumerate(fft_of(terms, -1)):
            work[first, rows] = re.astype(bf16)
            work[first, lower] = im.astype(bf16)
        return carry

    lax.fori_loop(0, LINES // step, spread_lines, 0)

    def one_residue(first, carry):
        spectrum = jnp.dot(forward[first], work[first], preferred_element_type=f32)
        re, im = spectrum[:LINES], spectrum[LINES:]
        gre, gim = filt[first, :LINES], filt[first, LINES:]
        filtered = jnp.concatenate([re * gre - im * gim, re * gim + im * gre], 0).astype(bf16)
        planes[first] = jnp.dot(backward[first], filtered, preferred_element_type=f32)
        return carry

    lax.fori_loop(0, PARTS, one_residue, 0)

    def gather_lines(chunk, carry):
        rows = pl.ds(pl.multiple_of(chunk * step, step), step)
        lower = pl.ds(pl.multiple_of(chunk * step + LINES, step), step)
        terms = [(planes[first, rows], planes[first, lower]) for first in range(PARTS)]
        for j, (re, im) in enumerate(fft_of(terms, 1)):
            out_ref[j, 0, rows] = re.astype(bf16)
            out_ref[j, 1, rows] = im.astype(bf16)
        return carry

    lax.fori_loop(0, LINES // step, gather_lines, 0)

    for part in range(2):
        zero = jnp.zeros((8, COLS), f32)
        for j in range(PARTS):
            below = out_ref[j - 1, part, 48:64].astype(f32)[8:] if j > 0 else zero
            above = out_ref[j + 1, part, 0:16].astype(f32)[:8] if j < PARTS - 1 else zero
            out_ref[j, part, LINES:ROWS] = jnp.concatenate([below, above], 0).astype(bf16)


MESH = pl.DeviceIdType.MESH
HALF = 16


class Place:
    def __init__(self):
        self.date, self.swath = lax.axis_index("date"), lax.axis_index("swath")
        self.side, self.spot = self.date // HALF, self.date % HALF

    def departure(self, turn):
        return (self.swath + 1 + turn) % PARTS

    def arrival(self, turn):
        return (self.swath + PARTS - turn) % PARTS


def send(source, target, leaves, lands, date, swath):
    pltpu.make_async_remote_copy(
        source, target, leaves, lands, device_id=(date, swath), device_id_type=MESH
    ).start()


def drain(block, sem):
    pltpu.make_async_copy(block, block, sem).wait()


def tell(date, swath):
    barrier = pltpu.get_barrier_semaphore()
    pl.semaphore_signal(barrier, inc=1, device_id=(date, swath), device_id_type=MESH)


def greet(place):
    def each(turn, carry):
        tell(place.date, (place.swath + turn) % PARTS)
        return carry

    lax.fori_loop(1, PARTS, each, 0)

    @pl.when(place.spot != HALF - 1)
    def _():
        tell(place.date + 1, place.swath)

    for lane in range(2):

        @pl.when(place.spot != lane)
        def _():
            tell(HALF * place.side + lane, place.swath)

    @pl.when(place.spot == HALF - 1)
    def _():
        def every(part, carry):
            tell(HALF * (1 - place.side) + (place.swath + part) % HALF, part)
            return carry

        lax.fori_loop(0, PARTS, every, 0)


def await_greetings(place):
    wanted = (
        PARTS
        + jnp.where(place.spot != 0, 1, 0)
        + jnp.where(place.spot <= 1, HALF - 1, 0)
    )
    pl.semaphore_wait(pltpu.get_barrier_semaphore(), wanted)


def focus_kernel(
    rate_ref,
    offset_ref,
    frac_ref,
    echo_ref,
    rate_row,
    forward,
    backward,
    own,
    following,
    after,
    table,
    extended,
    leaving,
    columns,
    filt,
    work,
    planes,
    blocks,
    crossing,
    turn_send,
    turn_recv,
    back_send,
    back_recv,
    wrap_send,
    wrap_recv,
    next_send,
    next_recv,
    last_send,
    last_recv,
    tail_send,
):
    place = Place()
    greet(place)
    chirp_table(rate_ref[0], table)
    for part in range(2):
        rows = slice(LINES * part, LINES * (part + 1))
        extended[rows, :RG] = echo_ref[part]
        extended[rows, RG:] = echo_ref[part, :, :PULSE]

    def one_block(block, carry):
        window = extended[:, pl.ds(pl.multiple_of(block * WIDE, WIDE), DEPTH)]
        product = jnp.dot(window, table[...], preferred_element_type=f32)
        real = product[:LINES, :WIDE] - product[LINES:, WIDE:]
        imag = product[:LINES, WIDE:] + product[LINES:, :WIDE]
        for half in range(2):
            cols = slice(COLS * half, COLS * (half + 1))
            leaving[2 * block + half, 0] = real[:, cols].astype(bf16)
            leaving[2 * block + half, 1] = imag[:, cols].astype(bf16)
        return carry

    lax.fori_loop(0, RG // WIDE, one_block, 0)
    await_greetings(place)

    def hand_over(turn, carry):
        goal = place.departure(turn)
        send(leaving.at[goal], columns.at[place.swath], turn_send, turn_recv, place.date, goal)
        return carry

    lax.fori_loop(0, PARTS - 1, hand_over, 0)
    kept = leaving.at[place.swath]
    pltpu.make_async_copy(kept, columns.at[place.swath], turn_recv).start()
    azimuth_filter(rate_row[...], frac_ref[0], offset_ref[0], filt)
    drain(columns, turn_recv)
    drain(leaving.at[pl.ds(0, PARTS - 1)], turn_send)

    azimuth_focus(columns, filt, forward, backward, work, planes, blocks)

    side, spot, date, swath = place.side, place.spot, place.date, place.swath
    leads = spot <= 1
    lane = spot % 2

    @pl.when(leads)
    def _():
        def scatter(part, carry):
            goal = (swath + part) % HALF

            @pl.when(goal != spot)
            def _():
                send(
                    blocks.at[part],
                    crossing.at[lane],
                    wrap_send,
                    wrap_recv.at[lane],
                    HALF * side + goal,
                    swath,
                )

            @pl.when(goal == spot)
            def _():
                pltpu.make_async_copy(
                    blocks.at[part], crossing.at[lane], wrap_recv.at[lane]
                ).start()

            return carry

        lax.fori_loop(0, PARTS, scatter, 0)

    def hand_back(turn, carry):
        goal = place.departure(turn)
        send(blocks.at[goal], own.at[swath], back_send, back_recv.at[swath], date, goal)
        return carry

    lax.fori_loop(0, PARTS - 1, hand_back, 0)
    pltpu.make_async_copy(blocks.at[swath], own.at[swath], back_recv.at[swath]).start()

    for which, target, lands in ((0, following, next_recv.at[swath]), (1, after, last_recv)):
        drain(crossing.at[which], wrap_recv.at[which])
        send(
            crossing.at[which],
            target.at[swath],
            tail_send.at[which],
            lands,
            HALF * (1 - side) + HALF - 1,
            (spot + HALF - swath) % HALF,
        )

    has_next = spot != HALF - 1
    has_back = spot != 0
    delay = 2

    def relay(piece):
        drain(following.at[piece], next_recv.at[piece])

        @pl.when(has_back)
        def _():
            send(following.at[piece], after.at[piece], last_send, last_recv, date - 1, swath)

    def pass_on(turn, carry):
        @pl.when(turn < PARTS)
        def _():
            piece = place.arrival(turn % PARTS)
            drain(own.at[piece], back_recv.at[piece])

            @pl.when(has_back)
            def _():
                send(
                    own.at[piece],
                    following.at[piece],
                    next_send,
                    next_recv.at[piece],
                    date - 1,
                    swath,
                )

        @pl.when((turn >= delay) & has_next)
        def _():
            relay(place.arrival((turn + PARTS - delay) % PARTS))

        return carry

    lax.fori_loop(0, PARTS + delay, pass_on, 0)

    @pl.when(spot == HALF - 1)
    def _():
        def late(turn, carry):
            relay(place.arrival(turn))
            return carry

        lax.fori_loop(0, PARTS, late, 0)

    drain(after, last_recv)
    drain(blocks.at[pl.ds(0, PARTS - 1)], back_send)

    @pl.when(leads)
    def _():
        drain(blocks.at[pl.ds(0, HALF - 1)], wrap_send)

    @pl.when(has_back)
    def _():
        drain(own, next_send)
        drain(following, last_send)

    for which in range(2):
        drain(crossing.at[which], tail_send.at[which])


def line_sums():
    line = np.arange(LINES)[:, None]
    row = np.arange(ROWS)[None, :]
    place = np.where(row < LINES, row, np.where(row < LINES + 8, row - LINES - 8, row - 8))
    return (np.abs(place - line) <= WIN_AZ // 2).astype(np.float32)


def sample_sums():
    sample = np.arange(2 * WIDE)[:, None]
    middle = np.arange(WIDE)[None, :] + PAD
    return (np.abs(sample - middle) <= WIN_RG // 2).astype(np.float32)


def coherence_kernel(
    lines_ref, samples_ref, own_ref, next_ref, after_ref, image_ref, result_ref, held
):
    edge = jnp.zeros((7 * LINES, PAD), bf16)
    held[:, :PAD] = edge
    held[:, PAD + RG :] = edge
    sums = lines_ref[...]

    def one_piece(piece, carry):
        are, aim = own_ref[piece, 0].astype(f32), own_ref[piece, 1].astype(f32)
        maps = [are * are + aim * aim]
        for other in (next_ref, after_ref):
            bre, bim = other[piece, 0].astype(f32), other[piece, 1].astype(f32)
            maps += [bre * bre + bim * bim, are * bre + aim * bim, aim * bre - are * bim]
        lanes = pl.ds(pl.multiple_of(piece * COLS, COLS), COLS)
        stacked = jnp.concatenate([m.astype(bf16) for m in maps], 1)
        summed = jnp.dot(sums, stacked, preferred_element_type=f32)
        inner = pl.ds(pl.multiple_of(piece * COLS + PAD, COLS), COLS)
        for which in range(7):
            held[LINES * which : LINES * (which + 1), inner] = summed[
                :, COLS * which : COLS * (which + 1)
            ].astype(bf16)
        for part in range(2):
            image_ref[0, part, :, lanes] = own_ref[piece, part, :LINES]
        return carry

    lax.fori_loop(0, PARTS, one_piece, 0)

    def one_span(span, carry):
        start = pl.multiple_of(span * WIDE, WIDE)
        window = held[:, pl.ds(start, 2 * WIDE)]
        boxes = jnp.dot(window, samples_ref[...], preferred_element_type=f32)
        box = [boxes[LINES * which : LINES * (which + 1)] for which in range(7)]
        for pair in range(SPAN):
            scale = lax.rsqrt(box[0] * box[3 * pair + 1] + epsilon)
            for part in range(2):
                term = box[3 * pair + 2 + part] * scale
                result_ref[0, pair, part, :, pl.ds(start, WIDE)] = term.astype(bf16)
        return carry

    lax.fori_loop(0, RG // WIDE, one_span, 0)


def vmem(count):
    return [pl.BlockSpec(memory_space=pltpu.VMEM)] * count


def params(**more):
    return pltpu.CompilerParams(vmem_limit_bytes=56 * 1024 * 1024, **more)


def coherence_call(own, following, after):
    return pl.pallas_call(
        coherence_kernel,
        out_shape=(
            jax.ShapeDtypeStruct((1, 2, LINES, RG), bf16),
            jax.ShapeDtypeStruct((1, SPAN, 2, LINES, RG), bf16),
        ),
        in_specs=vmem(5),
        out_specs=tuple(vmem(2)),
        scratch_shapes=[pltpu.VMEM((7 * LINES, RG + 2 * PAD), bf16)],
        compiler_params=params(),
    )(
        jnp.asarray(line_sums(), bf16),
        jnp.asarray(sample_sums(), bf16),
        own,
        following,
        after,
    )


def focus_call(raw_echo, range_rate, azimuth_rate, line_offset, frac_shift):
    forward, backward = mini_dft()
    dma = pltpu.SemaphoreType.DMA
    return pl.pallas_call(
        focus_kernel,
        out_shape=(jax.ShapeDtypeStruct((PARTS, 2, ROWS, COLS), bf16),) * 3,
        in_specs=[pl.BlockSpec(memory_space=pltpu.SMEM)] * 3 + vmem(4),
        out_specs=tuple(vmem(3)),
        scratch_shapes=[
            pltpu.VMEM((DEPTH, 2 * WIDE), bf16),
            pltpu.VMEM((2 * LINES, RG + PULSE), bf16),
            pltpu.VMEM((PARTS, 2, LINES, COLS), bf16),
            pltpu.VMEM((PARTS, 2, LINES, COLS), bf16),
            pltpu.VMEM((PARTS, 2 * LINES, COLS), f32),
            pltpu.VMEM((PARTS, 2 * LINES, COLS), bf16),
            pltpu.VMEM((PARTS, 2 * LINES, COLS), f32),
            pltpu.VMEM((PARTS, 2, ROWS, COLS), bf16),
            pltpu.VMEM((2, 2, ROWS, COLS), bf16),
            dma,
            dma,
            dma,
            dma((PARTS,)),
            dma,
            dma((2,)),
            dma,
            dma((PARTS,)),
            dma,
            dma,
            dma((2,)),
        ],
        compiler_params=params(collective_id=0, has_side_effects=True),
    )(
        range_rate.reshape(1),
        line_offset,
        frac_shift,
        raw_echo[0],
        azimuth_rate.reshape(1, COLS),
        jnp.asarray(forward, bf16),
        jnp.asarray(backward, bf16),
    )


def body(raw_echo, range_rate, azimuth_rate, line_offset, frac_shift):
    return coherence_call(
        *focus_call(raw_echo, range_rate, azimuth_rate, line_offset, frac_shift)
    )


def solution(mesh):
    placed = (P("date", None, "swath", None), P(), P("swath"), P("date"), P("date"))
    return jax.shard_map(
        body,
        mesh=mesh,
        in_specs=placed,
        out_specs=(P("date", None, "swath", None), P("date", None, None, "swath", None)),
        check_vma=False,
    )
```

time: 144 us -> 110 us (0.76)
  the two profiles are of different devices: /device:TPU:62 before, /device:TPU:164 now
where the time goes in v2:
time: 110 us
  Pallas kernels  108 us (98%)
  between operations  2.57 us (2%)
    pallas_call x1, Pallas kernels, focus_call(): pl.pallas_call(focus_kernel, out_shape=(jax.ShapeDtypeStruct((PARTS, 2, R...  99.9 us
    pallas_call x1, Pallas kernels, coherence_call(): pl.pallas_call(coherence_kernel, out_shape=(jax.ShapeDtypeStruct((1, 2, L...  7.84 us

profile of v2, /device:TPU:164, one launch (start us, length us, event | category | flops | bytes accessed | tf_op | source)
XLA Modules:
  0.0 110.3 jit_solution(5619389286578448687)
XLA Ops:
  2.6 99.9 %shard_map.104 = (bf16[16,2,80,128]{3,2,1,0:T(8,128)(2,1)}, bf16[16,2,80,128]{3,2,1,0:T(8,128)(2,1)}, bf16[16,2,80,128]{3,2,1,0:T(8,128)(2,1)}) custom-call(f32[1]{0:T(128)} %bitcast.3.rate_ref, s32[1]{0:T(128)S(6)} %copy.12.offset_ref, f32[1]{0:T(128)S(6)} %copy.13.frac_ref, bf16[2,64,2048]{2,1,0:T(8,128)(2,1)} %bitcast.4, f32[1,128]{1,0:T(1,128)} %bitcast.5, ...), custom_call_target="tpu_custom_call" | custom-call | tf_op jit(solution)/shard_map/pallas_call | solution.py:492
  102.4 7.8 %shard_map.105 = (bf16[1,2,64,2048]{3,2,1,0:T(8,128)(2,1)}, bf16[1,2,2,64,2048]{4,3,2,1,0:T(8,128)(2,1)}) custom-call(bf16[64,80]{1,0:T(8,128)(2,1)} %constant.10.clone.lines_ref, bf16[512,256]{1,0:T(8,128)(2,1)} %constant.11.clone.samples_ref, bf16[16,2,80,128]{3,2,1,0:T(8,128)(2,1)} %get-tuple-element.5.own_ref, ...), custom_call_target="tpu_custom_call" | custom-call | tf_op jit(solution)/shard_map/pallas_call | solution.py:470

commit v3 on v2

--- a/solution.py
+++ b/solution.py
@@ -19,6 +19,11 @@
 LINES = AZ // PARTS
 COLS = RG // PARTS
 ROWS = LINES + 16
+TILE = 16
+WAVES = LINES // TILE
+ORDER = (0, WAVES - 1) + tuple(range(1, WAVES - 1))
+STRIDES = (8, 7, 4, 1, 15, 9, 10, 5, 2, 14, 6, 11, 12, 3, 13)
+AHEAD = 5
 PULSE = RG // 2
 WIDE = 256
 DEPTH = PULSE + WIDE
@@ -114,8 +119,8 @@
     lax.fori_loop(0, PARTS, one_residue, (jnp.cos(base), jnp.sin(base)))
 
 
-def azimuth_focus(columns, filt, forward, backward, work, planes, out_ref):
-    step = 16
+def azimuth_focus(columns, filt, forward, backward, work, planes):
+    step = TILE
 
     def spread_lines(chunk, carry):
         rows = pl.ds(pl.multiple_of(chunk * step, step), step)
@@ -138,25 +143,15 @@
         planes[first] = jnp.dot(backward[first], filtered, preferred_element_type=f32)
         return carry
 
-    lax.fori_loop(0, PARTS, one_residue, 0)
-
-    def gather_lines(chunk, carry):
-        rows = pl.ds(pl.multiple_of(chunk * step, step), step)
-        lower = pl.ds(pl.multiple_of(chunk * step + LINES, step), step)
-        terms = [(planes[first, rows], planes[first, lower]) for first in range(PARTS)]
-        for j, (re, im) in enumerate(fft_of(terms, 1)):
-            out_ref[j, 0, rows] = re.astype(bf16)
-            out_ref[j, 1, rows] = im.astype(bf16)
-        return carry
-
-    lax.fori_loop(0, LINES // step, gather_lines, 0)
-
-    for part in range(2):
-        zero = jnp.zeros((8, COLS), f32)
-        for j in range(PARTS):
-            below = out_ref[j - 1, part, 48:64].astype(f32)[8:] if j > 0 else zero
-            above = out_ref[j + 1, part, 0:16].astype(f32)[:8] if j < PARTS - 1 else zero
-            out_ref[j, part, LINES:ROWS] = jnp.concatenate([below, above], 0).astype(bf16)
+    lax.fori_loop(0, PARTS, one_residue, 0, unroll=4)
+
+
+def gather_lines(wave, planes, blocks):
+    rows, lower = pl.ds(TILE * wave, TILE), pl.ds(TILE * wave + LINES, TILE)
+    terms = [(planes[first, rows], planes[first, lower]) for first in range(PARTS)]
+    for j, (re, im) in enumerate(fft_of(terms, 1)):
+        blocks[wave, j, 0] = re.astype(bf16)
+        blocks[wave, j, 1] = im.astype(bf16)
 
 
 MESH = pl.DeviceIdType.MESH
@@ -197,9 +192,11 @@
 
     lax.fori_loop(1, PARTS, each, 0)
 
-    @pl.when(place.spot != HALF - 1)
-    def _():
-        tell(place.date + 1, place.swath)
+    for ahead in (1, 2):
+
+        @pl.when(place.spot < HALF - ahead)
+        def _():
+            tell(place.date + ahead, place.swath)
 
     for lane in range(2):
 
@@ -207,7 +204,7 @@
         def _():
             tell(HALF * place.side + lane, place.swath)
 
-    @pl.when(place.spot == HALF - 1)
+    @pl.when(place.spot >= HALF - 2)
     def _():
         def every(part, carry):
             tell(HALF * (1 - place.side) + (place.swath + part) % HALF, part)
@@ -219,7 +216,9 @@
 def await_greetings(place):
     wanted = (
         PARTS
+        + 1
         + jnp.where(place.spot != 0, 1, 0)
+        + jnp.where(place.spot >= 2, 1, 0)
         + jnp.where(place.spot <= 1, HALF - 1, 0)
     )
     pl.semaphore_wait(pltpu.get_barrier_semaphore(), wanted)
@@ -236,6 +235,7 @@
     own,
     following,
     after,
+    rims,
     table,
     extended,
     leaving,
@@ -256,9 +256,18 @@
     last_send,
     last_recv,
     tail_send,
+    rim_send,
+    rim_recv,
 ):
     place = Place()
     greet(place)
+    for which in range(SPAN + 1):
+        for edge in range(2):
+
+            @pl.when(place.swath == (PARTS - 1) * edge)
+            def _():
+                rims[which, edge] = jnp.zeros((PARTS, 2, TILE, COLS), bf16)
+
     chirp_table(rate_ref[0], table)
     for part in range(2):
         rows = slice(LINES * part, LINES * (part + 1))
@@ -276,7 +285,7 @@
             leaving[2 * block + half, 1] = imag[:, cols].astype(bf16)
         return carry
 
-    lax.fori_loop(0, RG // WIDE, one_block, 0)
+    lax.fori_loop(0, RG // WIDE, one_block, 0, unroll=2)
     await_greetings(place)
 
     def hand_over(turn, carry):
@@ -291,21 +300,25 @@
     drain(columns, turn_recv)
     drain(leaving.at[pl.ds(0, PARTS - 1)], turn_send)
 
-    azimuth_focus(columns, filt, forward, backward, work, planes, blocks)
+    azimuth_focus(columns, filt, forward, backward, work, planes)
 
     side, spot, date, swath = place.side, place.spot, place.date, place.swath
     leads = spot <= 1
     lane = spot % 2
+
+    for wave in range(WAVES):
+        gather_lines(wave, planes, blocks)
 
     @pl.when(leads)
     def _():
         def scatter(part, carry):
             goal = (swath + part) % HALF
+            piece = blocks.at[:, part]
 
             @pl.when(goal != spot)
             def _():
                 send(
-                    blocks.at[part],
+                    piece,
                     crossing.at[lane],
                     wrap_send,
                     wrap_recv.at[lane],
@@ -315,91 +328,110 @@
 
             @pl.when(goal == spot)
             def _():
-                pltpu.make_async_copy(
-                    blocks.at[part], crossing.at[lane], wrap_recv.at[lane]
-                ).start()
+                pltpu.make_async_copy(piece, crossing.at[lane], wrap_recv.at[lane]).start()
 
             return carry
 
         lax.fori_loop(0, PARTS, scatter, 0)
 
-    def hand_back(turn, carry):
-        goal = place.departure(turn)
-        send(blocks.at[goal], own.at[swath], back_send, back_recv.at[swath], date, goal)
-        return carry
-
-    lax.fori_loop(0, PARTS - 1, hand_back, 0)
-    pltpu.make_async_copy(blocks.at[swath], own.at[swath], back_recv.at[swath]).start()
-
-    for which, target, lands in ((0, following, next_recv.at[swath]), (1, after, last_recv)):
-        drain(crossing.at[which], wrap_recv.at[which])
-        send(
-            crossing.at[which],
-            target.at[swath],
-            tail_send.at[which],
-            lands,
-            HALF * (1 - side) + HALF - 1,
-            (spot + HALF - swath) % HALF,
-        )
-
-    has_next = spot != HALF - 1
+    def hand_back(stride):
+        goal = (swath + stride) % PARTS
+        send(blocks.at[:, goal], own.at[:, swath], back_send, back_recv.at[swath], date, goal)
+
+    for stride in STRIDES[:AHEAD]:
+        hand_back(stride)
+    pltpu.make_async_copy(blocks.at[:, swath], own.at[:, swath], back_recv.at[swath]).start()
+
     has_back = spot != 0
-    delay = 2
-
-    def relay(piece):
-        drain(following.at[piece], next_recv.at[piece])
-
+    has_second = spot >= 2
+
+    def pass_on(piece):
         @pl.when(has_back)
         def _():
-            send(following.at[piece], after.at[piece], last_send, last_recv, date - 1, swath)
-
-    def pass_on(turn, carry):
-        @pl.when(turn < PARTS)
+            send(own.at[:, piece], following.at[:, piece], next_send, next_recv, date - 1, swath)
+
+        @pl.when(has_second)
         def _():
-            piece = place.arrival(turn % PARTS)
-            drain(own.at[piece], back_recv.at[piece])
-
-            @pl.when(has_back)
+            send(own.at[:, piece], after.at[:, piece], last_send, last_recv, date - 2, swath)
+
+    def share_rim(which, source, wave):
+        edge = 1 if wave == 0 else 0
+
+        @pl.when(swath != (0 if wave == 0 else PARTS - 1))
+        def _():
+            send(
+                source.at[wave],
+                rims.at[which, edge],
+                rim_send.at[edge],
+                rim_recv.at[which, edge],
+                date,
+                swath - 1 if wave == 0 else swath + 1,
+            )
+
+    goal_line = (spot + HALF - swath) % HALF
+    deliveries = (
+        (0, following, next_recv, HALF - 1),
+        (1, after, last_recv, HALF - 1),
+        (0, after, last_recv, HALF - 2),
+    )
+
+    def deliver():
+        for which in range(2):
+            drain(crossing.at[which], wrap_recv.at[which])
+        for index, (which, target, lands, goal) in enumerate(deliveries):
+            send(
+                crossing.at[which],
+                target.at[:, swath],
+                tail_send.at[index],
+                lands,
+                HALF * (1 - side) + goal,
+                goal_line,
+            )
+
+    for turn, stride in enumerate((0,) + STRIDES):
+        piece = (swath + PARTS - stride) % PARTS
+        drain(own.at[:, piece], back_recv.at[piece])
+        if 0 < turn and turn + AHEAD <= len(STRIDES):
+            hand_back(STRIDES[turn + AHEAD - 1])
+        if turn == 3:
+            deliver()
+        pass_on(piece)
+    drain_order = ((0, own, None), (1, following, next_recv), (2, after, last_recv))
+    for which, image, lands in drain_order:
+        if lands is not None:
+            drain(image, lands)
+        for wave in ORDER[:2]:
+            share_rim(which, image, wave)
+
+    for which in range(SPAN + 1):
+        for edge in range(2):
+
+            @pl.when(swath != (PARTS - 1) * edge)
             def _():
-                send(
-                    own.at[piece],
-                    following.at[piece],
-                    next_send,
-                    next_recv.at[piece],
-                    date - 1,
-                    swath,
-                )
-
-        @pl.when((turn >= delay) & has_next)
-        def _():
-            relay(place.arrival((turn + PARTS - delay) % PARTS))
-
-        return carry
-
-    lax.fori_loop(0, PARTS + delay, pass_on, 0)
-
-    @pl.when(spot == HALF - 1)
-    def _():
-        def late(turn, carry):
-            relay(place.arrival(turn))
-            return carry
-
-        lax.fori_loop(0, PARTS, late, 0)
-
-    drain(after, last_recv)
-    drain(blocks.at[pl.ds(0, PARTS - 1)], back_send)
+                drain(rims.at[which, edge], rim_recv.at[which, edge])
+
+    drain(blocks.at[:, pl.ds(0, PARTS - 1)], back_send)
 
     @pl.when(leads)
     def _():
-        drain(blocks.at[pl.ds(0, HALF - 1)], wrap_send)
+        drain(blocks.at[:, pl.ds(0, HALF - 1)], wrap_send)
 
     @pl.when(has_back)
     def _():
         drain(own, next_send)
-        drain(following, last_send)
-
-    for which in range(2):
-        drain(crossing.at[which], tail_send.at[which])
+
+    @pl.when(has_second)
+    def _():
+        drain(own, last_send)
+
+    for index, (which, target, lands, goal) in enumerate(deliveries):
+        drain(crossing.at[which], tail_send.at[index])
+
+    for edge in range(2):
+
+        @pl.when(swath != (PARTS - 1) * (1 - edge))
+        def _():
+            drain(own.at[pl.ds(0, SPAN + 1)], rim_send.at[edge])
 
 
 def line_sums():
@@ -416,7 +448,15 @@
 
 
 def coherence_kernel(
-    lines_ref, samples_ref, own_ref, next_ref, after_ref, image_ref, result_ref, held
+    lines_ref,
+    samples_ref,
+    own_ref,
+    next_ref,
+    after_ref,
+    rims_ref,
+    image_ref,
+    result_ref,
+    held,
 ):
     edge = jnp.zeros((7 * LINES, PAD), bf16)
     held[:, :PAD] = edge
@@ -424,10 +464,16 @@
     sums = lines_ref[...]
 
     def one_piece(piece, carry):
-        are, aim = own_ref[piece, 0].astype(f32), own_ref[piece, 1].astype(f32)
+        def lines_of(which, image, part):
+            tiles = [image[wave, piece, part].astype(f32) for wave in range(WAVES)]
+            tiles.append(rims_ref[which, 0, piece, part].astype(f32)[8:])
+            tiles.append(rims_ref[which, 1, piece, part].astype(f32)[:8])
+            return jnp.concatenate(tiles, 0)
+
+        are, aim = lines_of(0, own_ref, 0), lines_of(0, own_ref, 1)
         maps = [are * are + aim * aim]
-        for other in (next_ref, after_ref):
-            bre, bim = other[piece, 0].astype(f32), other[piece, 1].astype(f32)
+        for which, other in ((1, next_ref), (2, after_ref)):
+            bre, bim = lines_of(which, other, 0), lines_of(which, other, 1)
             maps += [bre * bre + bim * bim, are * bre + aim * bim, aim * bre - are * bim]
         lanes = pl.ds(pl.multiple_of(piece * COLS, COLS), COLS)
         stacked = jnp.concatenate([m.astype(bf16) for m in maps], 1)
@@ -438,10 +484,12 @@
                 :, COLS * which : COLS * (which + 1)
             ].astype(bf16)
         for part in range(2):
-            image_ref[0, part, :, lanes] = own_ref[piece, part, :LINES]
-        return carry
-
-    lax.fori_loop(0, PARTS, one_piece, 0)
+            for wave in range(WAVES):
+                rows = slice(TILE * wave, TILE * (wave + 1))
+                image_ref[0, part, rows, lanes] = own_ref[wave, piece, part]
+        return carry
+
+    lax.fori_loop(0, PARTS, one_piece, 0, unroll=4)
 
     def one_span(span, carry):
         start = pl.multiple_of(span * WIDE, WIDE)
@@ -455,7 +503,7 @@
                 result_ref[0, pair, part, :, pl.ds(start, WIDE)] = term.astype(bf16)
         return carry
 
-    lax.fori_loop(0, RG // WIDE, one_span, 0)
+    lax.fori_loop(0, RG // WIDE, one_span, 0, unroll=2)
 
 
 def vmem(count):
@@ -466,14 +514,14 @@
     return pltpu.CompilerParams(vmem_limit_bytes=56 * 1024 * 1024, **more)
 
 
-def coherence_call(own, following, after):
+def coherence_call(own, following, after, rims):
     return pl.pallas_call(
         coherence_kernel,
         out_shape=(
             jax.ShapeDtypeStruct((1, 2, LINES, RG), bf16),
             jax.ShapeDtypeStruct((1, SPAN, 2, LINES, RG), bf16),
         ),
-        in_specs=vmem(5),
+        in_specs=vmem(6),
         out_specs=tuple(vmem(2)),
         scratch_shapes=[pltpu.VMEM((7 * LINES, RG + 2 * PAD), bf16)],
         compiler_params=params(),
@@ -483,6 +531,7 @@
         own,
         following,
         after,
+        rims,
     )
 
 
@@ -491,9 +540,10 @@
     dma = pltpu.SemaphoreType.DMA
     return pl.pallas_call(
         focus_kernel,
-        out_shape=(jax.ShapeDtypeStruct((PARTS, 2, ROWS, COLS), bf16),) * 3,
+        out_shape=(jax.ShapeDtypeStruct((WAVES, PARTS, 2, TILE, COLS), bf16),) * 3
+        + (jax.ShapeDtypeStruct((SPAN + 1, 2, PARTS, 2, TILE, COLS), bf16),),
         in_specs=[pl.BlockSpec(memory_space=pltpu.SMEM)] * 3 + vmem(4),
-        out_specs=tuple(vmem(3)),
+        out_specs=tuple(vmem(4)),
         scratch_shapes=[
             pltpu.VMEM((DEPTH, 2 * WIDE), bf16),
             pltpu.VMEM((2 * LINES, RG + PULSE), bf16),
@@ -502,8 +552,8 @@
             pltpu.VMEM((PARTS, 2 * LINES, COLS), f32),
             pltpu.VMEM((PARTS, 2 * LINES, COLS), bf16),
             pltpu.VMEM((PARTS, 2 * LINES, COLS), f32),
-            pltpu.VMEM((PARTS, 2, ROWS, COLS), bf16),
-            pltpu.VMEM((2, 2, ROWS, COLS), bf16),
+            pltpu.VMEM((WAVES, PARTS, 2, TILE, COLS), bf16),
+            pltpu.VMEM((2, WAVES, 2, TILE, COLS), bf16),
             dma,
             dma,
             dma,
@@ -511,10 +561,12 @@
             dma,
             dma((2,)),
             dma,
-            dma((PARTS,)),
-            dma,
-            dma,
+            dma,
+            dma,
+            dma,
+            dma((3,)),
             dma((2,)),
+            dma((SPAN + 1, 2)),
         ],
         compiler_params=params(collective_id=0, has_side_effects=True),
     )(

time: 110 us -> 101 us (0.918)
  the two profiles are of different devices: /device:TPU:164 before, /device:TPU:25 now
where the time goes in v3:
time: 101 us
  Pallas kernels  98.5 us (98%)
  between operations  2.57 us (3%)
    pallas_call x1, Pallas kernels, focus_call(): pl.pallas_call(focus_kernel, out_shape=(jax.ShapeDtypeStruct((WAVES, PART...  92.6 us
    pallas_call x1, Pallas kernels, coherence_call(): pl.pallas_call(coherence_kernel, out_shape=(jax.ShapeDtypeStruct((1, 2, L...  5.84 us

profile of v3, /device:TPU:25, one launch (start us, length us, event | category | flops | bytes accessed | tf_op | source)
XLA Modules:
  0.0 101.0 jit_solution(9323784031430340092)
XLA Ops:
  2.6 92.6 %shard_map.104 = (bf16[4,16,2,16,128]{4,3,2,1,0:T(8,128)(2,1)}, bf16[4,16,2,16,128]{4,3,2,1,0:T(8,128)(2,1)}, bf16[4,16,2,16,128]{4,3,2,1,0:T(8,128)(2,1)}, bf16[3,2,16,2,16,128]{5,4,3,2,1,0:T(8,128)(2,1)}) custom-call(f32[1]{0:T(128)} %bitcast.3.rate_ref, s32[1]{0:T(128)S(6)} %copy.12.offset_ref, f32[1]{0:T(128)S(6)} %copy.13.frac_ref, ...), custom_call_target="tpu_custom_call" | custom-call | tf_op jit(solution)/shard_map/pallas_call | solution.py:541
  95.2 5.8 %shard_map.105 = (bf16[1,2,64,2048]{3,2,1,0:T(8,128)(2,1)}, bf16[1,2,2,64,2048]{4,3,2,1,0:T(8,128)(2,1)}) custom-call(bf16[64,80]{1,0:T(8,128)(2,1)} %constant.10.clone.lines_ref, bf16[512,256]{1,0:T(8,128)(2,1)} %constant.11.clone.samples_ref, bf16[4,16,2,16,128]{4,3,2,1,0:T(8,128)(2,1)} %get-tuple-element.6.own_ref, ...), custom_call_target="tpu_custom_call" | custom-call | tf_op jit(solution)/shard_map/pallas_call | solution.py:518

commit v4 on v3

--- a/solution.py
+++ b/solution.py
@@ -143,7 +143,7 @@
         planes[first] = jnp.dot(backward[first], filtered, preferred_element_type=f32)
         return carry
 
-    lax.fori_loop(0, PARTS, one_residue, 0, unroll=4)
+    lax.fori_loop(0, PARTS, one_residue, 0, unroll=8)
 
 
 def gather_lines(wave, planes, blocks):
@@ -285,7 +285,7 @@
             leaving[2 * block + half, 1] = imag[:, cols].astype(bf16)
         return carry
 
-    lax.fori_loop(0, RG // WIDE, one_block, 0, unroll=2)
+    lax.fori_loop(0, RG // WIDE, one_block, 0, unroll=4)
     await_greetings(place)
 
     def hand_over(turn, carry):
@@ -489,7 +489,7 @@
                 image_ref[0, part, rows, lanes] = own_ref[wave, piece, part]
         return carry
 
-    lax.fori_loop(0, PARTS, one_piece, 0, unroll=4)
+    lax.fori_loop(0, PARTS, one_piece, 0, unroll=8)
 
     def one_span(span, carry):
         start = pl.multiple_of(span * WIDE, WIDE)
@@ -503,7 +503,7 @@
                 result_ref[0, pair, part, :, pl.ds(start, WIDE)] = term.astype(bf16)
         return carry
 
-    lax.fori_loop(0, RG // WIDE, one_span, 0, unroll=2)
+    lax.fori_loop(0, RG // WIDE, one_span, 0, unroll=4)
 
 
 def vmem(count):

time: 101 us -> 100 us (0.990)
  the two profiles are of different devices: /device:TPU:25 before, /device:TPU:9 now
where the time goes in v4:
time: 100 us; the launch traced here: 99.8 us
  Pallas kernels  97.2 us (97%)
  between operations  2.57 us (3%)
    pallas_call x1, Pallas kernels, focus_call(): pl.pallas_call(focus_kernel, out_shape=(jax.ShapeDtypeStruct((WAVES, PART...  91.9 us
    pallas_call x1, Pallas kernels, coherence_call(): pl.pallas_call(coherence_kernel, out_shape=(jax.ShapeDtypeStruct((1, 2, L...  5.27 us

profile of v4, /device:TPU:9, one launch (start us, length us, event | category | flops | bytes accessed | tf_op | source)
XLA Modules:
  0.0 99.8 jit_solution(8411604898664022685)
XLA Ops:
  2.6 91.9 %shard_map.104 = (bf16[4,16,2,16,128]{4,3,2,1,0:T(8,128)(2,1)}, bf16[4,16,2,16,128]{4,3,2,1,0:T(8,128)(2,1)}, bf16[4,16,2,16,128]{4,3,2,1,0:T(8,128)(2,1)}, bf16[3,2,16,2,16,128]{5,4,3,2,1,0:T(8,128)(2,1)}) custom-call(f32[1]{0:T(128)} %bitcast.3.rate_ref, s32[1]{0:T(128)S(6)} %copy.12.offset_ref, f32[1]{0:T(128)S(6)} %copy.13.frac_ref, ...), custom_call_target="tpu_custom_call" | custom-call | tf_op jit(solution)/shard_map/pallas_call | solution.py:541
  94.5 5.3 %shard_map.105 = (bf16[1,2,64,2048]{3,2,1,0:T(8,128)(2,1)}, bf16[1,2,2,64,2048]{4,3,2,1,0:T(8,128)(2,1)}) custom-call(bf16[64,80]{1,0:T(8,128)(2,1)} %constant.10.clone.lines_ref, bf16[512,256]{1,0:T(8,128)(2,1)} %constant.11.clone.samples_ref, bf16[4,16,2,16,128]{4,3,2,1,0:T(8,128)(2,1)} %get-tuple-element.6.own_ref, ...), custom_call_target="tpu_custom_call" | custom-call | tf_op jit(solution)/shard_map/pallas_call | solution.py:518
